TPU v7x, 32 devices: a whole 2x2x4 slice. The times are simulated.
32 devices in a mesh: frames: 2 (over core), heads: 4 (over y, x), dp: 4 (over z).
Axes of the slice: x: 2, y: 2, z: 4, core: 2. Of those that a mesh axis runs over, the one named last changes fastest.
Arguments:
- queries: bfloat16 [1280, 4096], P(('dp', 'frames'), 'heads'), parts along dimension 0, may hold values from -10 to 10
- key_vectors: bfloat16 [1280, 4096], P(('dp', 'frames'), 'heads'), parts along dimension 0, may hold values from -4 to 4
- values: bfloat16 [1280, 4096], P(('dp', 'frames'), 'heads'), parts along dimension 0, may hold values from -5 to 5
- grad_output: bfloat16 [1280, 4096], P(('dp', 'frames'), 'heads'), parts along dimension 0, may hold values from -5 to 5
- segment_index: int32 [1280], P(('dp', 'frames')), parts along dimension 0, may hold values from 0 to 7, as said below
Outputs:
- attended: bfloat16 [1280, 4096], P(('dp', 'frames'), 'heads'), parts along dimension 0
- grad_queries: bfloat16 [1280, 4096], P(('dp', 'frames'), 'heads'), parts along dimension 0
- grad_keys: bfloat16 [1280, 4096], P(('dp', 'frames'), 'heads'), parts along dimension 0
- grad_values: bfloat16 [1280, 4096], P(('dp', 'frames'), 'heads'), parts along dimension 0
There are 4 independent parts, one for each index of `dp`. A program takes and returns all parts, laid end to end along the dimension named above; each array names one. Nothing has to cross between parts.
Inputs may be any that keep to these rules, and one draw needn't show every extreme that they name: `segment_index`: rows are stored in paired order: the first 80 rows of frames index g are the natural positions g * 80 onward, its last 80 rows the positions (3 - g) * 80 onward. Along natural positions the segment never falls, starts at 0 (the reference-image prefix), and each of the 8 segments holds at least one position.
All inputs are finite; a program needn't handle non-finite values.
Results may differ from a plain program's by a relative error of at most 0.014.
Values may be sent and summed in bfloat16 or wider, within the bound.
No kernel may reach another device: no remote copies, remote signals or barrier semaphores. Data moves between devices by JAX's collectives and lax.ppermute only.
A program may use at most 128 MiB of HBM per device.

v0:
```python
import math

import jax
import jax.numpy as jnp
from jax import lax
from jax.sharding import PartitionSpec as P

HEAD_DIM = 128


def head_split(array):
    return array.reshape(array.shape[0], array.shape[1] // HEAD_DIM, HEAD_DIM)


def natural_order(array, shard_count, row_count):
    half_rows = row_count // 2
    parts = array.reshape((shard_count, 2, half_rows) + array.shape[1:])
    joined = jnp.concatenate([parts[:, 0], jnp.flip(parts[:, 1], axis=0)], axis=0)
    return joined.reshape((shard_count * row_count,) + array.shape[1:])


def score_block(query_heads, key_heads):
    product = jnp.einsum("qhd,khd->qhk", query_heads, key_heads, preferred_element_type=jnp.float32)
    return product * (1.0 / math.sqrt(HEAD_DIM))


def visible(query_segment, key_segment):
    return key_segment[None, None, :] <= query_segment[:, None, None]


def weights_of(query_heads, query_segment, log_total, key_heads, key_segment):
    scores = score_block(query_heads, key_heads)
    return jnp.where(
        visible(query_segment, key_segment), jnp.exp(scores - log_total[:, :, None]), 0.0
    )


def grad_parts(
    query_heads,
    grad_heads,
    query_segment,
    log_total,
    row_delta,
    key_heads,
    value_heads,
    key_segment,
):
    soft_weights = weights_of(query_heads, query_segment, log_total, key_heads, key_segment)
    grad_weights = jnp.einsum(
        "qhd,khd->qhk", grad_heads, value_heads, preferred_element_type=jnp.float32
    )
    grad_scores = (soft_weights * (grad_weights - row_delta[:, :, None])).astype(jnp.bfloat16)
    return (soft_weights.astype(jnp.bfloat16), grad_scores)


def shards(queries, key_vectors, values, grad_output, segment_index):
    row_count, full_width = queries.shape
    head_count = full_width // HEAD_DIM
    shard_count = lax.axis_size("frames")
    scale_factor = 1.0 / math.sqrt(HEAD_DIM)
    query_heads = head_split(queries)
    grad_heads = head_split(grad_output)
    own_segment = segment_index.astype(jnp.float32)
    own_top = jnp.max(own_segment)
    own_bottom = jnp.min(own_segment)
    segment_tags = segment_index.astype(jnp.bfloat16)
    key_whole, value_whole, key_tags = (
        lax.all_gather(key_vectors, "frames", axis=0, tiled=True),
        lax.all_gather(values, "frames", axis=0, tiled=True),
        lax.all_gather(segment_tags, "frames", axis=0, tiled=True),
    )
    key_total = key_whole.shape[0]
    key_span = min(key_total, 4 * row_count)
    span_count = key_total // key_span
    key_heads_all = head_split(natural_order(key_whole, shard_count, row_count))
    value_heads_all = head_split(natural_order(value_whole, shard_count, row_count))
    key_segment_all = natural_order(key_tags, shard_count, row_count).astype(jnp.float32)

    def key_slice(block_index):
        first_row = block_index * key_span
        return (
            lax.dynamic_slice_in_dim(key_heads_all, first_row, key_span, 0),
            lax.dynamic_slice_in_dim(value_heads_all, first_row, key_span, 0),
            lax.dynamic_slice_in_dim(key_segment_all, first_row, key_span, 0),
        )

    def span_seen(key_segment):
        return jnp.min(key_segment) <= own_top

    def stats_step(block_index, loop_state):
        key_heads, value_heads, key_segment = key_slice(block_index)

        def stats_work(state):
            running_max, running_sum = state
            seen_mask = visible(own_segment, key_segment)
            scores = jnp.where(seen_mask, score_block(query_heads, key_heads), -1e30)
            new_max = jnp.maximum(running_max, jnp.max(scores, axis=2))
            added = jnp.sum(
                jnp.where(seen_mask, jnp.exp(scores - new_max[:, :, None]), 0.0), axis=2
            )
            return (new_max, running_sum * jnp.exp(running_max - new_max) + added)

        return lax.cond(span_seen(key_segment), stats_work, lambda state: state, loop_state)

    start_max = jnp.full((row_count, head_count), -1e30, jnp.float32)
    start_sum = jnp.zeros((row_count, head_count), jnp.float32)
    running_max, running_sum = lax.fori_loop(0, span_count, stats_step, (start_max, start_sum))
    log_total = running_max + jnp.log(running_sum)

    def output_step(block_index, total_acc):
        key_heads, value_heads, key_segment = key_slice(block_index)

        def output_work(acc):
            weights_low = weights_of(
                query_heads, own_segment, log_total, key_heads, key_segment
            ).astype(jnp.bfloat16)
            return acc + jnp.einsum(
                "qhk,khd->qhd", weights_low, value_heads, preferred_element_type=jnp.float32
            )

        return lax.cond(span_seen(key_segment), output_work, lambda acc: acc, total_acc)

    zero_rows = jnp.zeros((row_count, head_count, HEAD_DIM), jnp.float32)
    attended = (
        lax.fori_loop(0, span_count, output_step, zero_rows)
        .reshape(row_count, full_width)
        .astype(jnp.bfloat16)
    )
    row_delta = jnp.sum(
        grad_heads.astype(jnp.float32) * head_split(attended).astype(jnp.float32), axis=2
    )

    def query_grad_step(block_index, total_acc):
        key_heads, value_heads, key_segment = key_slice(block_index)

        def query_work(acc):
            weights_low, grad_scores = grad_parts(
                query_heads,
                grad_heads,
                own_segment,
                log_total,
                row_delta,
                key_heads,
                value_heads,
                key_segment,
            )
            return acc + jnp.einsum(
                "qhk,khd->qhd", grad_scores, key_heads, preferred_element_type=jnp.float32
            )

        return lax.cond(span_seen(key_segment), query_work, lambda acc: acc, total_acc)

    query_acc = lax.fori_loop(0, span_count, query_grad_step, zero_rows)
    grad_queries = (query_acc * scale_factor).reshape(row_count, full_width).astype(jnp.bfloat16)
    query_whole, grad_whole, query_tags = (
        lax.all_gather(queries, "frames", axis=0, tiled=True),
        lax.all_gather(grad_output, "frames", axis=0, tiled=True),
        lax.all_gather(segment_tags, "frames", axis=0, tiled=True),
    )
    total_whole, delta_whole = (
        lax.all_gather(log_total, "frames", axis=0, tiled=True),
        lax.all_gather(row_delta, "frames", axis=0, tiled=True),
    )
    query_heads_all = head_split(natural_order(query_whole, shard_count, row_count))
    grad_heads_all = head_split(natural_order(grad_whole, shard_count, row_count))
    query_segment_all = natural_order(query_tags, shard_count, row_count).astype(jnp.float32)
    total_all = natural_order(total_whole, shard_count, row_count)
    delta_all = natural_order(delta_whole, shard_count, row_count)
    own_keys = head_split(key_vectors)
    own_values = head_split(values)

    def key_grad_step(block_index, loop_state):
        first_row = block_index * key_span
        block_queries = lax.dynamic_slice_in_dim(query_heads_all, first_row, key_span, 0)
        block_grads = lax.dynamic_slice_in_dim(grad_heads_all, first_row, key_span, 0)
        block_segment = lax.dynamic_slice_in_dim(query_segment_all, first_row, key_span, 0)
        block_total = lax.dynamic_slice_in_dim(total_all, first_row, key_span, 0)
        block_delta = lax.dynamic_slice_in_dim(delta_all, first_row, key_span, 0)

        def key_work(state):
            key_acc, value_acc = state
            weights_low, grad_scores = grad_parts(
                block_queries,
                block_grads,
                block_segment,
                block_total,
                block_delta,
                own_keys,
                own_values,
                own_segment,
            )
            key_acc = key_acc + jnp.einsum(
                "qhk,qhd->khd", grad_scores, block_queries, preferred_element_type=jnp.float32
            )
            value_acc = value_acc + jnp.einsum(
                "qhk,qhd->khd", weights_low, block_grads, preferred_element_type=jnp.float32
            )
            return (key_acc, value_acc)

        return lax.cond(
            jnp.max(block_segment) >= own_bottom, key_work, lambda state: state, loop_state
        )

    key_acc, value_acc = lax.fori_loop(0, span_count, key_grad_step, (zero_rows, zero_rows))
    grad_keys = (key_acc * scale_factor).reshape(row_count, full_width).astype(jnp.bfloat16)
    grad_values = value_acc.reshape(row_count, full_width).astype(jnp.bfloat16)
    return (attended, grad_queries, grad_keys, grad_values)


def solution(mesh):
    in_specs = (
        P(("dp", "frames"), "heads"),
        P(("dp", "frames"), "heads"),
        P(("dp", "frames"), "heads"),
        P(("dp", "frames"), "heads"),
        P(("dp", "frames")),
    )
    out_specs = (
        P(("dp", "frames"), "heads"),
        P(("dp", "frames"), "heads"),
        P(("dp", "frames"), "heads"),
        P(("dp", "frames"), "heads"),
    )
    return jax.shard_map(shards, mesh=mesh, in_specs=in_specs, out_specs=out_specs, check_vma=False)
```

profile of v0, /device:TPU:13, one launch (start us, length us, event | category | flops | bytes accessed | tf_op | source)
XLA Modules:
  0.0 52.6 jit_solution(4312484970379094822)
XLA Ops:
  0.6 1.2 %dynamic-slice = u32[1]{0:T(128)} dynamic-slice(u32[32]{0:T(128)} %constant.59, u32[]{:T(128)S(6)} %add.42), dynamic_slice_sizes={1} | dynamic-slice | bytes 12
  2.5 1.3 %convert_reduce_fusion = (f32[]{:T(128)}, f32[]{:T(128)}) fusion(s32[160]{0:T(256)} %param.17), kind=kLoop, calls=%fused_computation.99 | loop fusion | flops 478 | bytes 648 | tf_op jit(solution)/shard_map/reduce_min | solution.py:65
  3.8 0.8 %fusion.69 = (f32[160]{0:T(256)S(1)}, bf16[160]{0:T(256)(128)(2,1)S(1)}) fusion(s32[160]{0:T(256)} %param.17), kind=kLoop, calls=%fused_computation.105 | loop fusion | flops 320 | bytes 1600 | tf_op jit(solution)/shard_map/convert_element_type | solution.py:63
  4.6 0.2 dynamic-update-slice
  4.8 2.8 %all-reduce = bf16[320]{0:T(512)(128)(2,1)S(1)} all-reduce(bf16[320]{0:T(512)(128)(2,1)S(1)} %dynamic-update-slice), channel_id=1, replica_groups=mesh['frames'=2,'heads'=4,'dp'=4] {'frames'}, use_global_device_ids=true, to_apply=%add | all-reduce | flops 320 | bytes 1280
  7.6 0.1 reshape.189
  7.6 0.6 %slice_reduce_fusion = (bf16[]{:T(256)}, bf16[2,1,80]{2,1,0:T(2,128)(2,1)S(1)}, bf16[2,1,80]{2,1,0:T(2,128)(2,1)S(1)}) fusion(bf16[2,2,80]{2,1,0:T(2,128)(2,1)S(1)} %reshape.189), kind=kLoop, calls=%fused_computation.102 | loop fusion | flops 159 | bytes 1282 | tf_op jit(solution)/shard_map/while/body/eval_jaxpr/reduce_max | solution.py:201
  8.3 0.6 %fusion.66 = f32[]{:T(128)} fusion(bf16[2,80]{1,0:T(2,128)(2,1)S(1)} %rev.25, bf16[2,80]{1,0:T(2,128)(2,1)S(1)} %get-tuple-element.446), kind=kLoop, calls=%fused_computation.101 | loop fusion | flops 1599 | bytes 644 | tf_op jit(solution)/shard_map/while/body/eval_jaxpr/reduce_min | solution.py:88
  10.2 0.6 %reduce_max.43 = bf16[]{:T(256)} reduce(bf16[2,80]{1,0:T(2,128)(2,1)S(1)} %rev.25, bf16[]{:T(256)} %constant.56.clone.1), dimensions={0,1}, to_apply=%region_12.13 | reduce | flops 159 | bytes 324 | tf_op jit(solution)/shard_map/while/body/eval_jaxpr/reduce_max | solution.py:201
  12.8 0.1 reshape.198
  12.9 1.0 %copy.149 = bf16[20,8,8,128]{3,2,1,0:T(8,128)(2,1)S(1)} copy(bf16[20,8,8,128]{3,1,2,0:T(8,128)(2,1)} %bitcast.200) | data formatting | bytes 655360
  13.9 0.0 copy-start.2
  13.9 1.8 %copy.146 = bf16[20,8,8,128]{3,2,1,0:T(8,128)(2,1)} copy(bf16[20,8,8,128]{3,1,2,0:T(8,128)(2,1)} %bitcast.199) | data formatting | bytes 655360
  15.7 2.5 %all_gather.25 = bf16[320,1024]{1,0:T(8,128)(2,1)S(1)} all-gather(bf16[160,1024]{1,0:T(8,128)(2,1)} %param.13), channel_id=1, replica_groups=mesh['frames'=2,'heads'=4,'dp'=4] {'frames'}, dimensions={0}, use_global_device_ids=true | all-gather | bytes 983040 | tf_op jit(solution)/shard_map/all_gather | solution.py:156
  18.3 0.0 copy-done.2
  18.3 2.3 %all_gather.23 = bf16[320,1024]{1,0:T(8,128)(2,1)S(1)} all-gather(bf16[160,1024]{1,0:T(8,128)(2,1)S(1)} %copy-done.2), channel_id=1, replica_groups=mesh['frames'=2,'heads'=4,'dp'=4] {'frames'}, dimensions={0}, use_global_device_ids=true | all-gather | bytes 983040 | tf_op jit(solution)/shard_map/all_gather | solution.py:68
  20.6 0.1 pad_maximum_fusion
  20.7 0.1 copy.145
  20.8 0.0 copy-start
  20.8 2.7 %conditional.4 = ((f32[160,8]{0,1:T(8,128)S(1)}, f32[160,8]{0,1:T(8,128)S(1)})) conditional(s32[]{:T(128)} %convert_element_type.80, (f32[160,8]{0,1:T(8,128)S(1)}, f32[160,8]{0,1:T(8,128)S(1)}) %tuple.64, (f32[320]{0:T(512)S(1)}, f32[160]{0:T(256)S(1)}, bf16[320,8,128]{2,1,0:T(8,128)(2,1)S(1)}, bf16[160,8,128]{2,1,0:T(8,128)(2,1)}, ...), branch_computations={%region_2.3_spmd, %region_3.6_spmd} | conditional | flops 108188160 | bytes 4481944 | solution.py:103
  20.9 0.1 broadcast_compare_fusion
  21.0 1.6 %fusion = (f32[160,8]{0,1:T(8,128)S(1)}, f32[8,320,160]{1,2,0:T(8,128)S(1)}) fusion(pred[160,320]{1,0:T(8,128)(4,1)S(1)} %broadcast_compare_fusion, bf16[160,8,128]{2,1,0:T(8,128)(2,1)} %get-tuple-element.392, bf16[320,8,128]{2,1,0:T(8,128)(2,1)S(1)} %get-tuple-element.391), kind=kOutput, calls=%fused_computation.2 | convolution fusion | flops 106085120 | bytes 2677760 | tf_op jit(solution)/shard_map/while/body/eval_jaxpr/cond/branch_1_fun/qhd,khd->qhk/dot_general | solution.py:23
  22.6 0.9 %select_reduce_fusion = f32[160,8]{0,1:T(8,128)S(1)} fusion(f32[8,320,160]{1,2,0:T(8,128)S(1)} %get-tuple-element.427, f32[160,8]{0,1:T(8,128)S(1)} %max.2, pred[160,320]{1,0:T(8,128)(4,1)S(1)} %broadcast_compare_fusion), kind=kLoop, calls=%fused_computation.1 | loop fusion | flops 2046720 | bytes 1699840 | tf_op jit(solution)/shard_map/while/body/eval_jaxpr/cond/branch_1_fun/reduce_sum | solution.py:98
  23.5 1.8 %all-gather = f32[2,160,8]{1,2,0:T(8,128)S(1)} all-gather(f32[1,160,8]{1,2,0:T(8,128)S(1)} %bitcast.208), channel_id=1, replica_groups=mesh['frames'=2,'heads'=4,'dp'=4] {'frames'}, dimensions={0}, use_global_device_ids=true | all-gather | bytes 15360 | tf_op jit(solution)/shard_map/all_gather | solution.py:161
  25.3 0.1 reshape.195
  25.5 0.0 copy-done
  25.5 2.3 %all_gather.24 = bf16[320,1024]{1,0:T(8,128)(2,1)S(1)} all-gather(bf16[160,1024]{1,0:T(8,128)(2,1)S(1)} %copy-done), channel_id=1, replica_groups=mesh['frames'=2,'heads'=4,'dp'=4] {'frames'}, dimensions={0}, use_global_device_ids=true | all-gather | bytes 983040 | tf_op jit(solution)/shard_map/all_gather | solution.py:69
  27.8 0.1 pad_maximum_fusion.1
  27.9 1.0 %copy.147 = bf16[40,8,8,128]{3,2,1,0:T(8,128)(2,1)} copy(bf16[40,8,8,128]{3,1,2,0:T(8,128)(2,1)S(1)} %bitcast.194) | data formatting | bytes 1310720
  28.9 2.2 %conditional.5 = (f32[160,8,128]{2,0,1:T(8,128)S(1)}) conditional(s32[]{:T(128)} %convert_element_type.80, f32[160,8,128]{2,0,1:T(8,128)S(1)} %broadcast_in_dim.72, (f32[320]{0:T(512)S(1)}, f32[160]{0:T(256)S(1)}, bf16[320,8,128]{2,1,0:T(8,128)(2,1)S(1)}, bf16[160,8,128]{2,1,0:T(8,128)(2,1)}, f32[160,8]{0,1:T(8,128)S(1)}, ...), branch_computations={%region_6.7_spmd, %region_7.8_spmd} | conditional | flops 211568640 | bytes 3058568 | solution.py:121
  28.9 0.1 broadcast_compare_fusion.1
  29.1 2.1 %fusion.9 = f32[160,8,128]{2,0,1:T(8,128)S(1)} fusion(f32[160,8,128]{2,0,1:T(8,128)S(1)} %get-tuple-element.230, f32[160,8]{0,1:T(8,128)S(1)} %get-tuple-element.248, pred[160,320]{1,0:T(8,128)(4,1)S(1)} %broadcast_compare_fusion.1, bf16[320,8,128]{2,1,0:T(8,128)(2,1)} %get-tuple-element.400, bf16[320,8,128]{2,1,0:T(8,128)(2,1)S(1)} %get-tuple-element.397, ...), kind=kOutput, calls=%fused_computation.14 | convolution fusion | flops 211517440 | bytes 3005440 | tf_op jit(solution)/shard_map/while/body/eval_jaxpr/cond/branch_1_fun/qhk,khd->qhd/dot_general | solution.py:117
  31.1 0.5 multiply_reduce_fusion
  31.6 0.8 %copy.205 = bf16[20,8,8,128]{3,1,2,0:T(8,128)(2,1)} copy(bf16[20,8,8,128]{3,2,1,0:T(8,128)(2,1)S(1)} %bitcast.203) | data formatting | bytes 655360
  32.4 0.0 copy-start.1
  32.4 5.8 %conditional.6 = (f32[160,8,128]{2,0,1:T(8,128)S(1)}) conditional(s32[]{:T(128)} %convert_element_type.80, f32[160,8,128]{2,0,1:T(8,128)S(1)} %broadcast_in_dim.72, (f32[320]{0:T(512)S(1)}, f32[160]{0:T(256)S(1)}, bf16[320,8,128]{2,1,0:T(8,128)(2,1)S(1)}, bf16[160,8,128]{2,1,0:T(8,128)(2,1)}, f32[160,8]{0,1:T(8,128)S(1)}, ...), branch_computations={%region_9.10_spmd, %region_10.11_spmd} | conditional | flops 317245440 | bytes 7333768 | solution.py:151
  32.4 0.1 copy.117
  32.5 0.1 broadcast_compare_fusion.2
  32.6 2.7 %fusion.35 = f32[8,320,160]{1,2,0:T(8,128)} fusion(bf16[320,8,128]{2,1,0:T(8,128)(2,1)S(1)} %get-tuple-element.404, bf16[160,8,128]{2,1,0:T(8,128)(2,1)} %get-tuple-element.405), kind=kOutput, calls=%fused_computation.40 | convolution fusion | flops 104857600 | bytes 2621440 | tf_op jit(solution)/shard_map/while/body/eval_jaxpr/cond/branch_1_fun/qhd,khd->qhk/dot_general | solution.py:23
  35.3 2.9 %fusion.27 = f32[160,8,128]{2,0,1:T(8,128)S(1)} fusion(f32[160,8,128]{2,0,1:T(8,128)S(1)} %get-tuple-element.250, f32[8,320,160]{1,2,0:T(8,128)} %fusion.35, f32[160,8]{0,1:T(8,128)S(1)} %copy.117, f32[160,8]{0,1:T(8,128)S(1)} %get-tuple-element.255, pred[160,320]{1,0:T(8,128)(4,1)S(1)} %broadcast_compare_fusion.2, ...), kind=kOutput, calls=%fused_computation.33 | convolution fusion | flops 212336640 | bytes 4648960 | tf_op jit(solution)/shard_map/while/body/eval_jaxpr/cond/branch_1_fun/qhk,khd->qhd/dot_general | solution.py:147
  38.2 0.8 %copy_bitcast_fusion.3 = bf16[160,1024]{1,0:T(8,128)(2,1)} fusion(f32[160,8,128]{2,0,1:T(8,128)S(1)} %get-tuple-element.459), kind=kLoop, calls=%fused_computation.83 | loop fusion | flops 327680 | bytes 983040 | tf_op jit(solution)/shard_map/convert_element_type | solution.py:154
  39.0 0.1 copy.122
  39.1 1.8 %all-gather.1 = f32[2,160,8]{1,2,0:T(8,128)S(1)} all-gather(f32[1,160,8]{1,2,0:T(8,128)S(1)} %copy.122), channel_id=1, replica_groups=mesh['frames'=2,'heads'=4,'dp'=4] {'frames'}, dimensions={0}, use_global_device_ids=true | all-gather | bytes 15360 | tf_op jit(solution)/shard_map/all_gather | solution.py:162
  40.9 0.1 reshape.197
  41.0 0.0 copy-done.1
  41.0 2.3 %all_gather.27 = bf16[320,1024]{1,0:T(8,128)(2,1)S(1)} all-gather(bf16[160,1024]{1,0:T(8,128)(2,1)S(1)} %copy-done.1), channel_id=1, replica_groups=mesh['frames'=2,'heads'=4,'dp'=4] {'frames'}, dimensions={0}, use_global_device_ids=true | all-gather | bytes 983040 | tf_op jit(solution)/shard_map/all_gather | solution.py:157
  43.4 0.1 pad_maximum_fusion.2
  43.5 6.5 %conditional.7 = (f32[160,8,128]{2,0,1:T(8,128)}, f32[160,8,128]{2,0,1:T(8,128)S(1)}) conditional(s32[]{:T(128)} %convert_element_type.89, f32[160,8,128]{2,0,1:T(8,128)S(1)} %broadcast_in_dim.72, (f32[160]{0:T(256)S(1)}, f32[320]{0:T(512)S(1)}, bf16[160,1024]{1,0:T(8,128)(2,1)}, bf16[4,80,1024]{2,1,0:T(8,128)(2,1)S(1)}, ...), branch_computations={%region_14.15_spmd, %region_15.16_spmd} | conditional | flops 422676480 | bytes 13641616 | solution.py:200
  43.6 0.1 reshape.179
  43.6 0.1 copy.141
  43.8 0.1 reshape.177
  43.9 0.1 broadcast_compare_fusion.3
  44.0 1.0 %copy.140 = bf16[40,8,8,128]{3,2,1,0:T(8,128)(2,1)} copy(bf16[40,8,8,128]{3,1,2,0:T(8,128)(2,1)S(1)} %bitcast.188) | data formatting | bytes 1310720 | tf_op jit(solution)/shard_map/while/body/eval_jaxpr/cond
  44.9 1.8 %fusion.46 = f32[320,8,160]{0,2,1:T(8,128)S(1)} fusion(f32[320,8]{0,1:T(8,128)S(1)} %reshape.177, pred[320,160]{0,1:T(8,128)(4,1)S(1)} %broadcast_compare_fusion.3, bf16[320,8,128]{2,1,0:T(8,128)(2,1)} %bitcast.53, bf16[160,1024]{1,0:T(8,128)(2,1)} %get-tuple-element.262), kind=kOutput, calls=%fused_computation.53 | convolution fusion | flops 106086400 | bytes 2682880 | tf_op jit(solution)/shard_map/while/body/eval_jaxpr/cond/branch_1_fun/qhd,khd->qhk/dot_general | solution.py:23
  46.7 2.8 %fusion.50 = f32[160,8,128]{2,0,1:T(8,128)} fusion(f32[160,8,128]{2,0,1:T(8,128)S(1)} %get-tuple-element.259, f32[320,8,160]{0,2,1:T(8,128)S(1)} %fusion.46, f32[320,8]{0,1:T(8,128)S(1)} %reshape.179, bf16[320,8,128]{2,1,0:T(8,128)(2,1)S(1)} %bitcast.186, bf16[320,8,128]{2,1,0:T(8,128)(2,1)} %bitcast.53, bf16[160,1024]{1,0:T(8,128)(2,1)} %get-tuple-element.265), kind=kOutput, calls=%fused_computation.58 | convolution fusion | flops 211107840 | bytes 4597760 | tf_op jit(solution)/shard_map/while/body/eval_jaxpr/cond/branch_1_fun/qhk,qhd->khd/dot_general | solution.py:192
  49.5 0.5 fusion.48
  50.0 1.9 %copy_bitcast_fusion.2 = bf16[160,1024]{1,0:T(8,128)(2,1)} fusion(f32[160,8,128]{2,0,1:T(8,128)} %get-tuple-element.278), kind=kLoop, calls=%fused_computation.82 | loop fusion | flops 327680 | bytes 983040 | tf_op jit(solution)/shard_map/convert_element_type | solution.py:205
  51.9 0.8 %copy_bitcast_fusion.1 = bf16[160,1024]{1,0:T(8,128)(2,1)} fusion(f32[160,8,128]{2,0,1:T(8,128)S(1)} %get-tuple-element.279), kind=kLoop, calls=%fused_computation.81 | loop fusion | flops 163840 | bytes 983040 | tf_op jit(solution)/shard_map/convert_element_type | solution.py:206
  (27 shorter events, 0.4 us)
Async XLA Ops:
  13.9 4.4 %copy-start.2 = (bf16[160,1024]{1,0:T(8,128)(2,1)S(1)}, bf16[160,1024]{1,0:T(8,128)(2,1)}, u32[]{:S(2)}) copy-start(bf16[160,1024]{1,0:T(8,128)(2,1)} %param.14) | copy-start | bytes 983044
  20.8 4.7 %copy-start = (bf16[160,1024]{1,0:T(8,128)(2,1)S(1)}, bf16[160,1024]{1,0:T(8,128)(2,1)}, u32[]{:S(2)}) copy-start(bf16[160,1024]{1,0:T(8,128)(2,1)} %param.15) | copy-start | bytes 983044
  32.4 8.6 %copy-start.1 = (bf16[160,1024]{1,0:T(8,128)(2,1)S(1)}, bf16[160,1024]{1,0:T(8,128)(2,1)}, u32[]{:S(2)}) copy-start(bf16[160,1024]{1,0:T(8,128)(2,1)} %param.16) | copy-start | bytes 983044
where the time goes:
time: 53.2 us; the launch traced here: 52.6 us
  blocking collectives  15.7 us (30%)
  matrix products  14.4 us (27%)
  other arithmetic  9.38 us (18%)
  local copies, waits for them, and re-layouts  8.24 us (15%)
  between operations  4.77 us (9%)
    unnamed x16, local copies, waits for them, and re-layouts  6.23 us
    dot_general x3, matrix products, score_block(): jnp.einsum('qhd,khd->qhk', query_heads, key_heads, preferred_element_type...  6.15 us
    dot_general x1, matrix products, query_work(): jnp.einsum('qhk,khd->qhd', grad_scores, key_heads, preferred_element_type...  2.92 us
    dot_general x1, matrix products, key_work(): jnp.einsum('qhk,qhd->khd', grad_scores, block_queries, preferred_element_...  2.78 us
    unnamed x1, blocking collectives  2.78 us
    all_gather x1, blocking collectives, shards(): lax.all_gather(queries, 'frames', axis=0, tiled=True)  2.47 us
    all_gather x1, blocking collectives, shards(): lax.all_gather(values, 'frames', axis=0, tiled=True)  2.28 us
    all_gather x1, blocking collectives, shards(): lax.all_gather(key_vectors, 'frames', axis=0, tiled=True)  2.28 us

commit v1 on v0

--- a/solution.py
+++ b/solution.py
@@ -1,8 +1,11 @@
+import functools
 import math
 
 import jax
 import jax.numpy as jnp
 from jax import lax
+from jax.experimental import pallas as pl
+from jax.experimental.pallas import tpu as pltpu
 from jax.sharding import PartitionSpec as P
 
 HEAD_DIM = 128
@@ -207,6 +210,72 @@
     return (attended, grad_queries, grad_keys, grad_values)
 
 
+HIDDEN = -1e30
+NT = (((1,), (1,)), ((), ()))
+TN = (((0,), (0,)), ((), ()))
+NN = (((1,), (0,)), ((), ()))
+
+
+def dot(left, right, dims):
+    return lax.dot_general(left, right, dims, preferred_element_type=jnp.float32)
+
+
+def pair_kernel(
+    head_count, row_count, bias_ref, q0, k0, v0, g0, q1, k1, v1, g1, o_ref, dq_ref, dk_ref, dv_ref
+):
+    scale = 1.0 / math.sqrt(HEAD_DIM)
+    for head in range(head_count):
+        cols = slice(head * HEAD_DIM, (head + 1) * HEAD_DIM)
+        q = jnp.concatenate([q0[:, cols], q1[:, cols]], axis=0)
+        k = jnp.concatenate([k0[:, cols], k1[:, cols]], axis=0)
+        v = jnp.concatenate([v0[:, cols], v1[:, cols]], axis=0)
+        g = jnp.concatenate([g0[:, cols], g1[:, cols]], axis=0)
+        scores = dot(k, q, NT) + bias_ref[...]
+        top = jnp.max(scores, axis=0, keepdims=True)
+        raw = jnp.exp((scores - top) * scale)
+        soft = raw * (1.0 / jnp.sum(raw, axis=0, keepdims=True))
+        low = soft.astype(jnp.bfloat16)
+        grad_weights = dot(v, g, NT)
+        product = soft * grad_weights
+        delta = jnp.sum(product, axis=0, keepdims=True)
+        grad_scores = (product - soft * delta).astype(jnp.bfloat16)
+        o_ref[:, cols] = dot(low[:, :row_count], v, TN).astype(jnp.bfloat16)
+        dq_ref[:, cols] = (dot(grad_scores[:, :row_count], k, TN) * scale).astype(jnp.bfloat16)
+        dk_ref[:, cols] = (dot(grad_scores[:row_count], q, NN) * scale).astype(jnp.bfloat16)
+        dv_ref[:, cols] = dot(low[:row_count], g, NN).astype(jnp.bfloat16)
+
+
+def pair_body(queries, key_vectors, values, grad_output, segment_index):
+    row_count, width = queries.shape
+
+    def swap(array):
+        return lax.ppermute(array, "frames", [(0, 1), (1, 0)])
+
+    other_segment = swap(segment_index)
+    other_queries, other_keys = swap(queries), swap(key_vectors)
+    other_values, other_grad = swap(values), swap(grad_output)
+    segment = jnp.concatenate([segment_index, other_segment])
+    bias = jnp.where(segment[:, None] <= segment[None, :], 0.0, HIDDEN).astype(jnp.float32)
+    out = jax.ShapeDtypeStruct((row_count, width), jnp.bfloat16)
+    whole = pl.BlockSpec(memory_space=pltpu.VMEM)
+    return pl.pallas_call(
+        functools.partial(pair_kernel, width // HEAD_DIM, row_count),
+        out_shape=(out,) * 4,
+        in_specs=[whole] * 9,
+        out_specs=(whole,) * 4,
+    )(
+        bias,
+        queries,
+        key_vectors,
+        values,
+        grad_output,
+        other_queries,
+        other_keys,
+        other_values,
+        other_grad,
+    )
+
+
 def solution(mesh):
     in_specs = (
         P(("dp", "frames"), "heads"),
@@ -221,4 +290,5 @@
         P(("dp", "frames"), "heads"),
         P(("dp", "frames"), "heads"),
     )
-    return jax.shard_map(shards, mesh=mesh, in_specs=in_specs, out_specs=out_specs, check_vma=False)
+    body = pair_body if mesh.shape["frames"] == 2 else shards
+    return jax.shard_map(body, mesh=mesh, in_specs=in_specs, out_specs=out_specs, check_vma=False)

time: 53.2 us -> 13.5 us (0.25)
  blocking collectives: 15.7 us -> 0 us
  matrix products: 14.4 us -> 0 us
  other arithmetic: 9.38 us -> 1.64 us
  Pallas kernels: 0 us -> 7.6 us
  local copies, waits for them, and re-layouts: 8.24 us -> 1.11 us
  between operations: 4.77 us -> 0.65 us
  starting transfers between devices: 0 us -> 1.76 us
  waiting for transfers between devices: 0 us -> 0.56 us
    dot_general x7 -> x0, matrix products: 14.4 us -> none  [the longest x3 6.15 us: score_block(): jnp.einsum('qhd,khd->qhk', query_heads, key_heads, preferred_element_type...]
    all_gather x6 -> x0, blocking collectives: 12.9 us -> none  [the longest x1 2.47 us: shards(): lax.all_gather(queries, 'frames', axis=0, tiled=True)]
    pallas_call x0 -> x1, Pallas kernels: none -> 7.6 us  [pair_body(): pl.pallas_call(functools.partial(pair_kernel, width // HEAD_DIM, row_coun...]
    unnamed x16 -> x8, local copies, waits for them, and re-layouts: 6.23 us -> 1.11 us
    convert_element_type x5 -> x0, other arithmetic: 4.21 us -> none  [the longest x1 1.88 us: shards(): (key_acc * scale_factor).reshape(row_count, full_width).astype(jnp.bfloat16)]
    unnamed x1 -> x0, blocking collectives: 2.78 us -> none
    reduce_min x2 -> x0, other arithmetic: 1.9 us -> none  [the longest x1 1.29 us: shards(): own_bottom = jnp.min(own_segment)]
    ppermute x0 -> x5, starting transfers between devices: none -> 1.76 us  [swap(): return lax.ppermute(array, 'frames', [(0, 1), (1, 0)])]
  transfers between devices with their start and end apart: 0 -> 5, of which waited for: 0 -> 2; matrix products, arithmetic and copies ran while one was open for 0% -> 12% of each run, Pallas kernels for 0% -> 0%
where the time goes in v1:
time: 13.5 us; the launch traced here: 13.3 us
  Pallas kernels  7.6 us (56%)
  starting transfers between devices  1.76 us (13%)
  other arithmetic  1.64 us (12%)
  local copies, waits for them, and re-layouts  1.11 us (8%)
  between operations  0.65 us (5%)
  waiting for transfers between devices  0.56 us (4%)
    pallas_call x1, Pallas kernels, pair_body(): pl.pallas_call(functools.partial(pair_kernel, width // HEAD_DIM, row_coun...  7.6 us
    ppermute x5, starting transfers between devices, swap(): return lax.ppermute(array, 'frames', [(0, 1), (1, 0)])  1.76 us
    unnamed x8, local copies, waits for them, and re-layouts  1.11 us
    select_n x1, other arithmetic, pair_body(): jnp.where(segment[:, None] <= segment[None, :], 0.0, HIDDEN)  0.89 us
    concatenate x1, other arithmetic, pair_body(): segment = jnp.concatenate([segment_index, other_segment])  0.75 us
    ppermute x5, waiting for transfers between devices, swap(): return lax.ppermute(array, 'frames', [(0, 1), (1, 0)])  0.56 us
  transfers between devices with their start and end apart: 5, of which 2 were waited for; matrix products, arithmetic and copies ran while one was open for 12% of the time, Pallas kernels for 0%

profile of v1, /device:TPU:13, one launch (start us, length us, event | category | flops | bytes accessed | tf_op | source)
XLA Modules:
  0.0 13.3 jit_solution(2214579390925475748)
XLA Ops:
  0.6 0.7 %collective-permute-start = (s32[160]{0:T(256)}, s32[160]{0:T(256)S(1)}, u32[]{:S(2)}, u32[]{:S(2)}) collective-permute-start(s32[160]{0:T(256)} %param.9), channel_id=1, source_target_pairs={{0,16},{16,0},{1,17},{17,1},{2,18},{18,2},{3,19},{19,3},{4,20},{20... | collective-permute-start | bytes 1928 | tf_op jit(solution)/shard_map/ppermute | solution.py:252
  1.4 0.1 collective-permute-start.1
  1.4 0.4 %collective-permute-start.2 = (bf16[160,1024]{1,0:T(8,128)(2,1)}, bf16[160,1024]{1,0:T(8,128)(2,1)S(1)}, u32[]{:S(2)}, u32[]{:S(2)}) collective-permute-start(bf16[160,1024]{1,0:T(8,128)(2,1)} %k0.1), channel_id=1, source_target_pairs={{0,16},{16,0},{1,17},{17,1},{2,18},{18,2},{3,19},{19,3},{4,20},{20... | collective-permute-start | bytes 983048 | tf_op jit(solution)/shard_map/ppermute | solution.py:252
  1.9 0.1 collective-permute-start.3
  2.0 0.4 %collective-permute-start.4 = (bf16[160,1024]{1,0:T(8,128)(2,1)}, bf16[160,1024]{1,0:T(8,128)(2,1)S(1)}, u32[]{:S(2)}, u32[]{:S(2)}) collective-permute-start(bf16[160,1024]{1,0:T(8,128)(2,1)} %g0.1), channel_id=1, source_target_pairs={{0,16},{16,0},{1,17},{17,1},{2,18},{18,2},{3,19},{19,3},{4,20},{20... | collective-permute-start | bytes 983048 | tf_op jit(solution)/shard_map/ppermute | solution.py:252
  2.4 0.0 collective-permute-done
  2.4 0.8 %pad_add_fusion = s32[320]{0:T(512)S(1)} fusion(s32[160]{0:T(256)S(1)} %collective-permute-done, s32[160]{0:T(256)} %param.9), kind=kLoop, calls=%fused_computation.1 | loop fusion | flops 320 | bytes 2560 | tf_op jit(solution)/shard_map/concatenate | solution.py:257
  3.2 0.9 %compare_select_fusion.bias_ref = f32[320,320]{1,0:T(8,128)} fusion(s32[320]{0:T(512)S(1)} %pad_add_fusion), kind=kLoop, calls=%fused_computation | loop fusion | flops 204800 | bytes 410880 | tf_op jit(solution)/shard_map/jit(_where)/select_n | solution.py:258
  4.0 0.0 collective-permute-done.1.q1
  4.0 0.0 copy-start
  4.0 0.0 collective-permute-done.2.k1
  4.1 0.0 copy-start.1
  4.1 0.1 collective-permute-done.3.v1
  4.1 0.0 copy-start.2
  4.2 0.5 %collective-permute-done.4.g1 = bf16[160,1024]{1,0:T(8,128)(2,1)S(1)} collective-permute-done((bf16[160,1024]{1,0:T(8,128)(2,1)}, bf16[160,1024]{1,0:T(8,128)(2,1)S(1)}, u32[]{:S(2)}, u32[]{:S(2)}) %collective-permute-start.4) | collective-permute-done | bytes 327712 | tf_op jit(solution)/shard_map/ppermute | solution.py:252
  4.6 0.1 %copy-done = bf16[160,1024]{1,0:T(8,128)(2,1)} copy-done((bf16[160,1024]{1,0:T(8,128)(2,1)}, bf16[160,1024]{1,0:T(8,128)(2,1)S(1)}, u32[]{:S(2)}) %copy-start) | copy-done | bytes 327704
  4.8 0.1 %copy-done.1 = bf16[160,1024]{1,0:T(8,128)(2,1)} copy-done((bf16[160,1024]{1,0:T(8,128)(2,1)}, bf16[160,1024]{1,0:T(8,128)(2,1)S(1)}, u32[]{:S(2)}) %copy-start.1) | copy-done | bytes 327704
  4.9 0.1 copy-done.2
  5.0 0.0 copy-start.3
  5.0 0.7 %copy-done.3 = bf16[160,1024]{1,0:T(8,128)(2,1)} copy-done((bf16[160,1024]{1,0:T(8,128)(2,1)}, bf16[160,1024]{1,0:T(8,128)(2,1)S(1)}, u32[]{:S(2)}) %copy-start.3) | copy-done | bytes 327704
  5.7 7.6 %shard_map.84 = (bf16[160,1024]{1,0:T(8,128)(2,1)}, bf16[160,1024]{1,0:T(8,128)(2,1)}, bf16[160,1024]{1,0:T(8,128)(2,1)}, bf16[160,1024]{1,0:T(8,128)(2,1)}) custom-call(f32[320,320]{1,0:T(8,128)} %compare_select_fusion.bias_ref, bf16[160,1024]{1,0:T(8,128)(2,1)} %q0.1, bf16[160,1024]{1,0:T(8,128)(2,1)} %k0.1, bf16[160,1024]{1,0:T(8,128)(2,1)} %v0.1, ...), custom_call_target="tpu_custom_call" | custom-call | tf_op jit(solution)/shard_map/pallas_call | solution.py:261
Async XLA Ops:
  0.6 1.8 %collective-permute-start = (s32[160]{0:T(256)}, s32[160]{0:T(256)S(1)}, u32[]{:S(2)}, u32[]{:S(2)}) collective-permute-start(s32[160]{0:T(256)} %param.9), channel_id=1, source_target_pairs={{0,16},{16,0},{1,17},{17,1},{2,18},{18,2},{3,19},{19,3},{4,20},{20... | collective-permute-start | bytes 1928 | tf_op jit(solution)/shard_map/ppermute | solution.py:252
  1.4 2.7 %collective-permute-start.1 = (bf16[160,1024]{1,0:T(8,128)(2,1)}, bf16[160,1024]{1,0:T(8,128)(2,1)S(1)}, u32[]{:S(2)}, u32[]{:S(2)}) collective-permute-start(bf16[160,1024]{1,0:T(8,128)(2,1)} %q0.1), channel_id=1, source_target_pairs={{0,16},{16,0},{1,17},{17,1},{2,18},{18,2},{3,19},{19,3},{4,20},{20... | collective-permute-start | bytes 983048 | tf_op jit(solution)/shard_map/ppermute | solution.py:252
  1.4 2.6 %collective-permute-start.2 = (bf16[160,1024]{1,0:T(8,128)(2,1)}, bf16[160,1024]{1,0:T(8,128)(2,1)S(1)}, u32[]{:S(2)}, u32[]{:S(2)}) collective-permute-start(bf16[160,1024]{1,0:T(8,128)(2,1)} %k0.1), channel_id=1, source_target_pairs={{0,16},{16,0},{1,17},{17,1},{2,18},{18,2},{3,19},{19,3},{4,20},{20... | collective-permute-start | bytes 983048 | tf_op jit(solution)/shard_map/ppermute | solution.py:252
  1.9 2.3 %collective-permute-start.3 = (bf16[160,1024]{1,0:T(8,128)(2,1)}, bf16[160,1024]{1,0:T(8,128)(2,1)S(1)}, u32[]{:S(2)}, u32[]{:S(2)}) collective-permute-start(bf16[160,1024]{1,0:T(8,128)(2,1)} %v0.1), channel_id=1, source_target_pairs={{0,16},{16,0},{1,17},{17,1},{2,18},{18,2},{3,19},{19,3},{4,20},{20... | collective-permute-start | bytes 983048 | tf_op jit(solution)/shard_map/ppermute | solution.py:252
  2.0 2.7 %collective-permute-start.4 = (bf16[160,1024]{1,0:T(8,128)(2,1)}, bf16[160,1024]{1,0:T(8,128)(2,1)S(1)}, u32[]{:S(2)}, u32[]{:S(2)}) collective-permute-start(bf16[160,1024]{1,0:T(8,128)(2,1)} %g0.1), channel_id=1, source_target_pairs={{0,16},{16,0},{1,17},{17,1},{2,18},{18,2},{3,19},{19,3},{4,20},{20... | collective-permute-start | bytes 983048 | tf_op jit(solution)/shard_map/ppermute | solution.py:252
  4.0 0.7 %copy-start = (bf16[160,1024]{1,0:T(8,128)(2,1)}, bf16[160,1024]{1,0:T(8,128)(2,1)S(1)}, u32[]{:S(2)}) copy-start(bf16[160,1024]{1,0:T(8,128)(2,1)S(1)} %collective-permute-done.1.q1) | copy-start | bytes 983044
  4.1 0.9 %copy-start.1 = (bf16[160,1024]{1,0:T(8,128)(2,1)}, bf16[160,1024]{1,0:T(8,128)(2,1)S(1)}, u32[]{:S(2)}) copy-start(bf16[160,1024]{1,0:T(8,128)(2,1)S(1)} %collective-permute-done.2.k1) | copy-start | bytes 983044
  4.1 0.9 %copy-start.2 = (bf16[160,1024]{1,0:T(8,128)(2,1)}, bf16[160,1024]{1,0:T(8,128)(2,1)S(1)}, u32[]{:S(2)}) copy-start(bf16[160,1024]{1,0:T(8,128)(2,1)S(1)} %collective-permute-done.3.v1) | copy-start | bytes 983044
  5.0 0.7 %copy-start.3 = (bf16[160,1024]{1,0:T(8,128)(2,1)}, bf16[160,1024]{1,0:T(8,128)(2,1)S(1)}, u32[]{:S(2)}) copy-start(bf16[160,1024]{1,0:T(8,128)(2,1)S(1)} %collective-permute-done.4.g1) | copy-start | bytes 983044

commit v2 on v0

--- a/solution.py
+++ b/solution.py
@@ -1,8 +1,11 @@
+import functools
 import math
 
 import jax
 import jax.numpy as jnp
 from jax import lax
+from jax.experimental import pallas as pl
+from jax.experimental.pallas import tpu as pltpu
 from jax.sharding import PartitionSpec as P
 
 HEAD_DIM = 128
@@ -207,6 +210,267 @@
     return (attended, grad_queries, grad_keys, grad_values)
 
 
+HIDDEN = -1e30
+LANES = 128
+CHUNK = 80
+NT = (((1,), (1,)), ((), ()))
+TN = (((0,), (0,)), ((), ()))
+NN = (((1,), (0,)), ((), ()))
+PLAN = ((("S", 0), ("M", 1)), (("P", 1), ("B", 2)), (("C", 4), ("E", 3)))
+
+
+def dot(left, right, dims):
+    return lax.dot_general(left, right, dims, preferred_element_type=jnp.float32)
+
+
+def cols(head, count=1):
+    return slice(head * HEAD_DIM, (head + count) * HEAD_DIM)
+
+
+def side_by_side(generators):
+    generators = list(generators)
+    while generators:
+        generators = [item for item in generators if next(item, None) is not None]
+
+
+def stack_rows(first, second, head, count=1):
+    return jnp.concatenate([first[:, cols(head, count)], second[:, cols(head, count)]], axis=0)
+
+
+def load_kernel(*refs):
+    count = (len(refs) - 1) // 2
+    copies = [
+        pltpu.make_async_copy(source, target, refs[-1].at[at])
+        for at, (source, target) in enumerate(zip(refs[:count], refs[count:]))
+    ]
+    for copy in copies:
+        copy.start()
+    for copy in copies:
+        copy.wait()
+
+
+def load_early(arrays):
+    arrays = tuple(pltpu.with_memory_space_constraint(array, pltpu.HBM) for array in arrays)
+    count = len(arrays)
+    return pl.pallas_call(
+        load_kernel,
+        out_shape=tuple(jax.ShapeDtypeStruct(array.shape, array.dtype) for array in arrays),
+        in_specs=[pl.BlockSpec(memory_space=pl.ANY)] * count,
+        out_specs=(pl.BlockSpec(memory_space=pltpu.VMEM),) * count,
+        scratch_shapes=[pltpu.SemaphoreType.DMA((count,))],
+        compiler_params=pltpu.CompilerParams(vmem_limit_bytes=4 * 1024 * 1024),
+        cost_estimate=pl.CostEstimate(
+            flops=0, transcendentals=0, bytes_accessed=2 * sum(a.size * 2 for a in arrays)
+        ),
+    )(*arrays)
+
+
+def pair_kernel(
+    heads, rows,
+    s0, s1, q0, k0, v0, g0, q1, k1, v1, g1,
+    o_hbm, dq_hbm, dk_hbm, dv_hbm,
+    bias_ref, o_ref, dq_ref, dk_ref, dv_ref, sem,
+):
+    scale = 1.0 / math.sqrt(HEAD_DIM)
+    scale_two = scale * math.log2(math.e)
+    total = 2 * rows
+    own_rest = rows - LANES
+    rest = 2 * own_rest
+    low_type = jnp.bfloat16
+
+    key_segment = jnp.concatenate([s0[...], s1[...]], axis=1)
+    tails = [s0[:, LANES:], s1[:, LANES:]]
+    query_segment = jnp.concatenate([s0[:, :LANES], s1[:, :LANES]] + tails + tails, axis=1)
+    key_column = jnp.transpose(jnp.broadcast_to(key_segment, (8, total)))[:, :1]
+    bias_ref[...] = jnp.where(key_column <= query_segment, 0.0, HIDDEN)
+
+    zero = jnp.zeros((rest, HEAD_DIM), low_type)
+
+    def tail_rows(first, second, head):
+        return jnp.concatenate([first[LANES:, cols(head)], second[LANES:, cols(head)]], axis=0)
+
+    def strip_rows(first, second, kind, head):
+        if kind == 0:
+            return first[:LANES, cols(head)]
+        if kind == 1:
+            return second[:LANES, cols(head)]
+        upper = jnp.concatenate([tail_rows(first, second, head), zero], axis=1)
+        lower = jnp.concatenate([zero, tail_rows(first, second, head + 1)], axis=1)
+        return jnp.concatenate([upper, lower], axis=0)
+
+    strips = []
+    for head in range(0, heads, 2):
+        strips += [(0, head), (1, head), (2, head), (0, head + 1), (1, head + 1)]
+    per_pair = 5
+    chunks = [(low, min(low + CHUNK, total)) for low in range(0, total, CHUNK)]
+    state = [dict() for _ in strips]
+    sums = {}
+    outputs = ((o_ref, o_hbm), (dq_ref, dq_hbm), (dk_ref, dk_hbm), (dv_ref, dv_hbm))
+
+    def fold(function, block):
+        return function(block.reshape(block.shape[0] // 8, 8, LANES), axis=0)
+
+    def add_to(name, head, part):
+        sums[name, head] = sums[name, head] + part if (name, head) in sums else part
+
+    def copy_out(at, head):
+        source, target = outputs[at]
+        span = cols(head, 2)
+        return pltpu.make_async_copy(
+            source.at[:, span], target.at[:, span], sem.at[at, head // 2]
+        )
+
+    def scores_stage(at):
+        kind, head = strips[at]
+        count = 2 if kind == 2 else 1
+        state[at]["s"] = dot(
+            stack_rows(k0, k1, head, count), strip_rows(q0, q1, kind, head), NT
+        )
+        yield True
+
+    def mask_stage(at):
+        kind, head = strips[at]
+        scores = state[at].pop("s")
+        masked, top = [], None
+        for low, high in chunks:
+            block = scores[low:high] + bias_ref[low:high, kind * LANES : (kind + 1) * LANES]
+            masked.append(block)
+            part = fold(jnp.max, block)
+            top = part if top is None else jnp.maximum(top, part)
+            yield True
+        state[at].update(masked=masked, top=jnp.max(top, axis=0, keepdims=True))
+
+    def products_stage(at):
+        kind, head = strips[at]
+        count = 2 if kind == 2 else 1
+        state[at]["dp"] = dot(
+            stack_rows(v0, v1, head, count), strip_rows(g0, g1, kind, head), NT
+        )
+        yield True
+
+    def softmax_stage(at):
+        top, masked, products = state[at].pop("top"), state[at].pop("masked"), state[at]["dp"]
+        raws, norm, delta = [], None, None
+        for (low, high), block in zip(chunks, masked):
+            raw = jnp.exp2((block - top) * scale_two)
+            raws.append(raw)
+            norm_part, delta_part = fold(jnp.sum, raw), fold(jnp.sum, raw * products[low:high])
+            norm = norm_part if norm is None else norm + norm_part
+            delta = delta_part if delta is None else delta + delta_part
+            yield True
+        inverse = 1.0 / jnp.sum(norm, axis=0, keepdims=True)
+        delta = jnp.sum(delta, axis=0, keepdims=True) * inverse
+        state[at].update(raws=raws, inverse=inverse, delta=delta)
+
+    def weights_stage(at):
+        kind, head = strips[at]
+        inverse, delta, raws, products = (
+            state[at].pop(name) for name in ("inverse", "delta", "raws", "dp")
+        )
+        weights, grads = [], []
+        for (low, high), raw in zip(chunks, raws):
+            if kind == 1 and low >= rows:
+                continue
+            soft = raw * inverse
+            weights.append(soft.astype(low_type))
+            grads.append((soft * (products[low:high] - delta)).astype(low_type))
+            yield True
+        state[at].update(
+            low=jnp.concatenate(weights, axis=0), ds=jnp.concatenate(grads, axis=0)
+        )
+
+    def outputs_stage(at):
+        kind, head = strips[at]
+        low, ds = state[at].pop("low"), state[at].pop("ds")
+        if kind < 2:
+            add_to("v", head, dot(low[:rows], strip_rows(g0, g1, kind, head), NN))
+            yield True
+            add_to("k", head, dot(ds[:rows], strip_rows(q0, q1, kind, head), NN))
+            yield True
+        if kind == 0:
+            o_ref[:LANES, cols(head)] = dot(low, stack_rows(v0, v1, head), TN).astype(low_type)
+            yield True
+            part = dot(ds, stack_rows(k0, k1, head), TN) * scale
+            dq_ref[:LANES, cols(head)] = part.astype(low_type)
+            yield True
+        if kind == 2:
+            for side in range(2):
+                span = cols(side)
+                add_to("v", head + side, dot(low[:rows], strip_rows(g0, g1, 2, head)[:, span], NN))
+                yield True
+                add_to("k", head + side, dot(ds[:rows], strip_rows(q0, q1, 2, head)[:, span], NN))
+                yield True
+            low_turned, ds_turned = jnp.transpose(low), jnp.transpose(ds)
+            for side in range(2):
+                mine = slice(side * rest, side * rest + own_rest)
+                span = cols(head + side)
+                part = dot(low_turned[mine], stack_rows(v0, v1, head + side), NN)
+                o_ref[LANES:, span] = part.astype(low_type)
+                part = dot(ds_turned[mine], stack_rows(k0, k1, head + side), NN) * scale
+                dq_ref[LANES:, span] = part.astype(low_type)
+                yield True
+        if at % per_pair == per_pair - 1:
+            for member in (head - 1, head):
+                dk_ref[:, cols(member)] = (sums.pop(("k", member)) * scale).astype(low_type)
+                dv_ref[:, cols(member)] = sums.pop(("v", member)).astype(low_type)
+            for output in range(len(outputs)):
+                copy_out(output, head - 1).start()
+        yield True
+
+    stages = dict(
+        S=scores_stage,
+        M=mask_stage,
+        P=products_stage,
+        B=softmax_stage,
+        E=weights_stage,
+        C=outputs_stage,
+    )
+    last_lag = max(lag for group in PLAN for _, lag in group)
+    for step in range(len(strips) + last_lag):
+        for group in PLAN:
+            side_by_side(
+                stages[name](step - lag) for name, lag in group if 0 <= step - lag < len(strips)
+            )
+    for head in range(0, heads, 2):
+        for output in range(len(outputs)):
+            copy_out(output, head).wait()
+
+
+def pair_body(queries, key_vectors, values, grad_output, segment_index):
+    rows, width = queries.shape
+    heads = width // HEAD_DIM
+
+    def swap(array):
+        return lax.ppermute(array, "frames", [(0, 1), (1, 0)])
+
+    other_keys, other_queries = swap(key_vectors), swap(queries)
+    other_values, other_grad = swap(values), swap(grad_output)
+    other_segment = swap(segment_index).reshape(1, rows)
+    own = load_early((segment_index.reshape(1, rows), queries, key_vectors, values, grad_output))
+    out = jax.ShapeDtypeStruct((rows, width), jnp.bfloat16)
+    on_chip = pl.BlockSpec(memory_space=pltpu.VMEM)
+    return pl.pallas_call(
+        functools.partial(pair_kernel, heads, rows),
+        out_shape=(out,) * 4,
+        in_specs=[on_chip] * 10,
+        out_specs=(pl.BlockSpec(memory_space=pl.ANY),) * 4,
+        scratch_shapes=[pltpu.VMEM((2 * rows, 3 * LANES), jnp.float32)]
+        + [pltpu.VMEM((rows, width), jnp.bfloat16)] * 4
+        + [pltpu.SemaphoreType.DMA((4, heads // 2))],
+        compiler_params=pltpu.CompilerParams(vmem_limit_bytes=32 * 1024 * 1024),
+    )(own[0], other_segment, *own[1:], other_queries, other_keys, other_values, other_grad)
+
+
+def pair_fits(rows, width):
+    return 4 * (rows - LANES) == LANES and width % (2 * HEAD_DIM) == 0
+
+
+def plan_for_shapes(queries, key_vectors, values, grad_output, segment_index):
+    paired = lax.axis_size("frames") == 2 and pair_fits(*queries.shape)
+    body = pair_body if paired else shards
+    return body(queries, key_vectors, values, grad_output, segment_index)
+
+
 def solution(mesh):
     in_specs = (
         P(("dp", "frames"), "heads"),
@@ -221,4 +485,6 @@
         P(("dp", "frames"), "heads"),
         P(("dp", "frames"), "heads"),
     )
-    return jax.shard_map(shards, mesh=mesh, in_specs=in_specs, out_specs=out_specs, check_vma=False)
+    return jax.shard_map(
+        plan_for_shapes, mesh=mesh, in_specs=in_specs, out_specs=out_specs, check_vma=False
+    )

time: 53.2 us -> 8.9 us (0.17)
  blocking collectives: 15.7 us -> 0 us
  matrix products: 14.4 us -> 0 us
  other arithmetic: 9.38 us -> 0 us
  local copies, waits for them, and re-layouts: 8.24 us -> 0 us
  Pallas kernels: 0 us -> 5.79 us
  between operations: 4.77 us -> 0.66 us
  starting transfers between devices: 0 us -> 1.76 us
    dot_general x7 -> x0, matrix products: 14.4 us -> none  [the longest x3 6.15 us: score_block(): jnp.einsum('qhd,khd->qhk', query_heads, key_heads, preferred_element_type...]
    all_gather x6 -> x0, blocking collectives: 12.9 us -> none  [the longest x1 2.47 us: shards(): lax.all_gather(queries, 'frames', axis=0, tiled=True)]
    unnamed x16 -> x0, local copies, waits for them, and re-layouts: 6.23 us -> none
    pallas_call x0 -> x2, Pallas kernels: none -> 5.79 us  [the longest x1 4.47 us: pair_body(): pl.pallas_call(functools.partial(pair_kernel, heads, rows), out_shape=(ou...]
    convert_element_type x5 -> x0, other arithmetic: 4.21 us -> none  [the longest x1 1.88 us: shards(): (key_acc * scale_factor).reshape(row_count, full_width).astype(jnp.bfloat16)]
    unnamed x1 -> x0, blocking collectives: 2.78 us -> none
    reduce_min x2 -> x0, other arithmetic: 1.9 us -> none  [the longest x1 1.29 us: shards(): own_bottom = jnp.min(own_segment)]
    ppermute x0 -> x5, starting transfers between devices: none -> 1.76 us  [swap(): return lax.ppermute(array, 'frames', [(0, 1), (1, 0)])]
  transfers between devices with their start and end apart: 0 -> 5, of which waited for: 0 -> 1; matrix products, arithmetic and copies ran while one was open for 0% -> 0% of each run, Pallas kernels for 0% -> 15%
where the time goes in v2:
time: 8.9 us; the launch traced here: 8.74 us
  Pallas kernels  5.79 us (65%)
  starting transfers between devices  1.76 us (20%)
  between operations  0.66 us (7%)
  waiting for transfers between devices  0.53 us (6%)
    pallas_call x1, Pallas kernels, pair_body(): pl.pallas_call(functools.partial(pair_kernel, heads, rows), out_shape=(ou...  4.47 us
    ppermute x5, starting transfers between devices, swap(): return lax.ppermute(array, 'frames', [(0, 1), (1, 0)])  1.76 us
    pallas_call x1, Pallas kernels, load_early(): pl.pallas_call(load_kernel, out_shape=tuple((jax.ShapeDtypeStruct(array.s...  1.33 us
    ppermute x5, waiting for transfers between devices, swap(): return lax.ppermute(array, 'frames', [(0, 1), (1, 0)])  0.53 us
  transfers between devices with their start and end apart: 5, of which 1 were waited for; matrix products, arithmetic and copies ran while one was open for 0% of the time, Pallas kernels for 15%

profile of v2, /device:TPU:13, one launch (start us, length us, event | category | flops | bytes accessed | tf_op | source)
XLA Modules:
  0.0 8.7 jit_solution(5951471282395845979)
XLA Ops:
  0.6 0.7 %collective-permute-start.1 = (bf16[160,1024]{1,0:T(8,128)(2,1)}, bf16[160,1024]{1,0:T(8,128)(2,1)S(1)}, u32[]{:S(2)}, u32[]{:S(2)}) collective-permute-start(bf16[160,1024]{1,0:T(8,128)(2,1)} %refs_1_.1), channel_id=1, source_target_pairs={{0,16},{16,0},{1,17},{17,1},{2,18},{18,2},{3,19},{19,3},{4,20},{20... | collective-permute-start | bytes 983048 | tf_op jit(solution)/shard_map/ppermute | solution.py:444
  1.4 0.1 collective-permute-start.2
  1.5 0.4 %collective-permute-start.3 = (bf16[160,1024]{1,0:T(8,128)(2,1)}, bf16[160,1024]{1,0:T(8,128)(2,1)S(1)}, u32[]{:S(2)}, u32[]{:S(2)}) collective-permute-start(bf16[160,1024]{1,0:T(8,128)(2,1)} %refs_3_.1), channel_id=1, source_target_pairs={{0,16},{16,0},{1,17},{17,1},{2,18},{18,2},{3,19},{19,3},{4,20},{20... | collective-permute-start | bytes 983048 | tf_op jit(solution)/shard_map/ppermute | solution.py:444
  1.9 0.1 collective-permute-start.4
  2.0 0.4 %collective-permute-start = (s32[160]{0:T(256)}, s32[160]{0:T(256)S(1)}, u32[]{:S(2)}, u32[]{:S(2)}) collective-permute-start(s32[160]{0:T(256)} %param.9), channel_id=1, source_target_pairs={{0,16},{16,0},{1,17},{17,1},{2,18},{18,2},{3,19},{19,3},{4,20},{20... | collective-permute-start | bytes 1928 | tf_op jit(solution)/shard_map/ppermute | solution.py:444
  2.4 1.3 %shard_map.84 = (s32[1,160]{1,0:T(1,128)S(1)}, bf16[160,1024]{1,0:T(8,128)(2,1)S(1)}, bf16[160,1024]{1,0:T(8,128)(2,1)S(1)}, bf16[160,1024]{1,0:T(8,128)(2,1)S(1)}, bf16[160,1024]{1,0:T(8,128)(2,1)S(1)}) custom-call(s32[1,160]{1,0:T(1,128)} %bitcast.3, bf16[160,1024]{1,0:T(8,128)(2,1)} %refs_1_.1, bf16[160,1024]{1,0:T(8,128)(2,1)} %refs_2_.1, ...), custom_call_target="tpu_custom_call" | custom-call | bytes 2622080 | tf_op jit(solution)/shard_map/pallas_call | solution.py:255
  3.7 0.5 %collective-permute-done = s32[160]{0:T(256)S(1)} collective-permute-done((s32[160]{0:T(256)}, s32[160]{0:T(256)S(1)}, u32[]{:S(2)}, u32[]{:S(2)}) %collective-permute-start) | collective-permute-done | bytes 672 | tf_op jit(solution)/shard_map/ppermute | solution.py:444
  4.2 0.0 collective-permute-done.1.q1
  4.2 0.0 collective-permute-done.2.k1
  4.3 0.0 collective-permute-done.3.v1
  4.3 0.0 collective-permute-done.4.g1
  4.3 4.5 %shard_map.85 = (bf16[160,1024]{1,0:T(8,128)(2,1)}, bf16[160,1024]{1,0:T(8,128)(2,1)}, bf16[160,1024]{1,0:T(8,128)(2,1)}, bf16[160,1024]{1,0:T(8,128)(2,1)}) custom-call(s32[1,160]{1,0:T(1,128)S(1)} %get-tuple-element.9.s0, s32[1,160]{1,0:T(1,128)S(1)} %bitcast.2, bf16[160,1024]{1,0:T(8,128)(2,1)S(1)} %get-tuple-element.10.q0, ...), custom_call_target="tpu_custom_call" | custom-call | tf_op jit(solution)/shard_map/pallas_call | solution.py:452
Async XLA Ops:
  0.6 3.6 %collective-permute-start.1 = (bf16[160,1024]{1,0:T(8,128)(2,1)}, bf16[160,1024]{1,0:T(8,128)(2,1)S(1)}, u32[]{:S(2)}, u32[]{:S(2)}) collective-permute-start(bf16[160,1024]{1,0:T(8,128)(2,1)} %refs_1_.1), channel_id=1, source_target_pairs={{0,16},{16,0},{1,17},{17,1},{2,18},{18,2},{3,19},{19,3},{4,20},{20... | collective-permute-start | bytes 983048 | tf_op jit(solution)/shard_map/ppermute | solution.py:444
  1.4 2.9 %collective-permute-start.2 = (bf16[160,1024]{1,0:T(8,128)(2,1)}, bf16[160,1024]{1,0:T(8,128)(2,1)S(1)}, u32[]{:S(2)}, u32[]{:S(2)}) collective-permute-start(bf16[160,1024]{1,0:T(8,128)(2,1)} %refs_2_.1), channel_id=1, source_target_pairs={{0,16},{16,0},{1,17},{17,1},{2,18},{18,2},{3,19},{19,3},{4,20},{20... | collective-permute-start | bytes 983048 | tf_op jit(solution)/shard_map/ppermute | solution.py:444
  1.5 2.8 %collective-permute-start.3 = (bf16[160,1024]{1,0:T(8,128)(2,1)}, bf16[160,1024]{1,0:T(8,128)(2,1)S(1)}, u32[]{:S(2)}, u32[]{:S(2)}) collective-permute-start(bf16[160,1024]{1,0:T(8,128)(2,1)} %refs_3_.1), channel_id=1, source_target_pairs={{0,16},{16,0},{1,17},{17,1},{2,18},{18,2},{3,19},{19,3},{4,20},{20... | collective-permute-start | bytes 983048 | tf_op jit(solution)/shard_map/ppermute | solution.py:444
  1.9 2.4 %collective-permute-start.4 = (bf16[160,1024]{1,0:T(8,128)(2,1)}, bf16[160,1024]{1,0:T(8,128)(2,1)S(1)}, u32[]{:S(2)}, u32[]{:S(2)}) collective-permute-start(bf16[160,1024]{1,0:T(8,128)(2,1)} %refs_4_.1), channel_id=1, source_target_pairs={{0,16},{16,0},{1,17},{17,1},{2,18},{18,2},{3,19},{19,3},{4,20},{20... | collective-permute-start | bytes 983048 | tf_op jit(solution)/shard_map/ppermute | solution.py:444
  2.0 2.3 %collective-permute-start = (s32[160]{0:T(256)}, s32[160]{0:T(256)S(1)}, u32[]{:S(2)}, u32[]{:S(2)}) collective-permute-start(s32[160]{0:T(256)} %param.9), channel_id=1, source_target_pairs={{0,16},{16,0},{1,17},{17,1},{2,18},{18,2},{3,19},{19,3},{4,20},{20... | collective-permute-start | bytes 1928 | tf_op jit(solution)/shard_map/ppermute | solution.py:444

commit v3 on v0

--- a/solution.py
+++ b/solution.py
@@ -1,8 +1,11 @@
+import functools
 import math
 
 import jax
 import jax.numpy as jnp
 from jax import lax
+from jax.experimental import pallas as pl
+from jax.experimental.pallas import tpu as pltpu
 from jax.sharding import PartitionSpec as P
 
 HEAD_DIM = 128
@@ -88,7 +91,7 @@
         return jnp.min(key_segment) <= own_top
 
     def stats_step(block_index, loop_state):
-        key_heads, value_heads, key_segment = key_slice(block_index)
+        key_heads, _, key_segment = key_slice(block_index)
 
         def stats_work(state):
             running_max, running_sum = state
@@ -134,7 +137,7 @@
         key_heads, value_heads, key_segment = key_slice(block_index)
 
         def query_work(acc):
-            weights_low, grad_scores = grad_parts(
+            _, grad_scores = grad_parts(
                 query_heads,
                 grad_heads,
                 own_segment,
@@ -207,6 +210,328 @@
     return (attended, grad_queries, grad_keys, grad_values)
 
 
+HIDDEN = -1e30
+LANES = 128
+CHUNK = 80
+NT = (((1,), (1,)), ((), ()))
+TN = (((0,), (0,)), ((), ()))
+NN = (((1,), (0,)), ((), ()))
+PLAN = ((("S", 0),), (("C", 5),), (("P", 0),), (("M", 1),), (("B", 2),), (("E", 3),))
+
+
+def dot(left, right, dims):
+    return lax.dot_general(left, right, dims, preferred_element_type=jnp.float32)
+
+
+def cols(head, count=1):
+    return slice(head * HEAD_DIM, (head + count) * HEAD_DIM)
+
+
+def side_by_side(generators):
+    generators = list(generators)
+    while generators:
+        generators = [item for item in generators if next(item, None) is not None]
+
+
+def stack_rows(first, second, head, count=1):
+    return jnp.concatenate([first[:, cols(head, count)], second[:, cols(head, count)]], axis=0)
+
+
+def load_kernel(*refs):
+    *sources, segment, stacked, own_segment, sem = refs
+    for at, source in enumerate(sources):
+        pltpu.make_async_copy(source, stacked.at[at], sem.at[0]).start()
+    segment_copy = pltpu.make_async_copy(segment, own_segment, sem.at[1])
+    segment_copy.start()
+    segment_copy.wait()
+    pltpu.make_async_copy(stacked, stacked, sem.at[0]).wait()
+
+
+def load_early(arrays, segment):
+    arrays = tuple(pltpu.with_memory_space_constraint(a, pltpu.HBM) for a in arrays + (segment,))
+    count = len(arrays)
+    stacked = jax.ShapeDtypeStruct((count - 1,) + arrays[0].shape, arrays[0].dtype)
+    return pl.pallas_call(
+        load_kernel,
+        out_shape=(stacked, jax.ShapeDtypeStruct(segment.shape, segment.dtype)),
+        in_specs=[pl.BlockSpec(memory_space=pl.ANY)] * count,
+        out_specs=(pl.BlockSpec(memory_space=pltpu.VMEM),) * 2,
+        scratch_shapes=[pltpu.SemaphoreType.DMA((2,))],
+        compiler_params=pltpu.CompilerParams(vmem_limit_bytes=4 * 1024 * 1024),
+        cost_estimate=pl.CostEstimate(
+            flops=0, transcendentals=0, bytes_accessed=4 * stacked.size
+        ),
+    )(*arrays)
+
+
+def fill_mask(bias_ref, s0, s1, query_segment):
+    key_segment = jnp.concatenate([s0[...], s1[...]], axis=1)
+    key_column = jnp.transpose(jnp.broadcast_to(key_segment, (8, key_segment.shape[1])))[:, :1]
+    bias_ref[...] = jnp.where(key_column <= query_segment, 0.0, HIDDEN)
+
+
+def run_strips(strips, rows, operands, bias_of, outputs_stage):
+    scale_two = math.log2(math.e) / math.sqrt(HEAD_DIM)
+    total = 2 * rows
+    q0, k0, v0, g0, q1, k1, v1, g1 = operands
+    chunks = [(low, min(low + CHUNK, total)) for low in range(0, total, CHUNK)]
+    state = [dict() for _ in strips]
+
+    def fold(function, block):
+        return function(block.reshape(block.shape[0] // 8, 8, LANES), axis=0)
+
+    def scores_stage(at):
+        kind, head = strips[at]
+        count = 2 if kind == "tail" else 1
+        state[at]["s"] = dot(
+            stack_rows(k0, k1, head, count), strip_rows(q0, q1, kind, head), NT
+        )
+        yield True
+
+    def mask_stage(at):
+        scores, bias = state[at].pop("s"), bias_of(strips[at][0])
+        masked, top = [], None
+        for low, high in chunks:
+            block = scores[low:high] + bias[low:high]
+            masked.append(block)
+            part = fold(jnp.max, block)
+            top = part if top is None else jnp.maximum(top, part)
+            yield True
+        state[at].update(masked=masked, top=jnp.max(top, axis=0, keepdims=True))
+
+    def products_stage(at):
+        kind, head = strips[at]
+        count = 2 if kind == "tail" else 1
+        state[at]["dp"] = dot(
+            stack_rows(v0, v1, head, count), strip_rows(g0, g1, kind, head), NT
+        )
+        yield True
+
+    def softmax_stage(at):
+        top, masked, products = state[at].pop("top"), state[at].pop("masked"), state[at]["dp"]
+        raws, norm, delta = [], None, None
+        for (low, high), block in zip(chunks, masked):
+            raw = jnp.exp2((block - top) * scale_two)
+            raws.append(raw)
+            norm_part, delta_part = fold(jnp.sum, raw), fold(jnp.sum, raw * products[low:high])
+            norm = norm_part if norm is None else norm + norm_part
+            delta = delta_part if delta is None else delta + delta_part
+            yield True
+        inverse = 1.0 / jnp.sum(norm, axis=0, keepdims=True)
+        delta = jnp.sum(delta, axis=0, keepdims=True) * inverse
+        state[at].update(raws=raws, inverse=inverse, delta=delta)
+
+    def weights_stage(at):
+        inverse, delta, raws, products = (
+            state[at].pop(name) for name in ("inverse", "delta", "raws", "dp")
+        )
+        weights, grads = [], []
+        for (low, high), raw in zip(chunks, raws):
+            if strips[at][0] == "other" and low >= rows:
+                continue
+            soft = raw * inverse
+            weights.append(soft.astype(jnp.bfloat16))
+            grads.append((soft * (products[low:high] - delta)).astype(jnp.bfloat16))
+            yield True
+        state[at].update(
+            low=jnp.concatenate(weights, axis=0), ds=jnp.concatenate(grads, axis=0)
+        )
+
+    def last_stage(at):
+        yield from outputs_stage(*strips[at], state[at].pop("low"), state[at].pop("ds"))
+
+    stages = dict(
+        S=scores_stage,
+        M=mask_stage,
+        P=products_stage,
+        B=softmax_stage,
+        E=weights_stage,
+        C=last_stage,
+    )
+    last_lag = max(lag for group in PLAN for _, lag in group)
+    for step in range(len(strips) + last_lag):
+        for group in PLAN:
+            side_by_side(
+                stages[name](step - lag) for name, lag in group if 0 <= step - lag < len(strips)
+            )
+
+
+def tail_rows(first, second, head):
+    return jnp.concatenate([first[LANES:, cols(head)], second[LANES:, cols(head)]], axis=0)
+
+
+def strip_rows(first, second, kind, head):
+    if kind == "own":
+        return first[:LANES, cols(head)]
+    if kind == "other":
+        return second[:LANES, cols(head)]
+    own, beside = tail_rows(first, second, head), tail_rows(first, second, head + 1)
+    zero = jnp.zeros_like(own)
+    upper = jnp.concatenate([own, zero], axis=1)
+    return jnp.concatenate([upper, jnp.concatenate([zero, beside], axis=1)], axis=0)
+
+
+def own_kernel(
+    heads, rows, s0, s1, own, k1, v1, o_ref, dq_ref, dk_ref, dv_ref, bias_ref
+):
+    q0, k0, v0, g0 = (own.at[at] for at in range(4))
+    scale = 1.0 / math.sqrt(HEAD_DIM)
+    fill_mask(bias_ref, s0, s1, s0[:, :LANES])
+
+    def outputs(kind, head, low, ds):
+        span = cols(head)
+        dv_ref[:, span] = dot(low[:rows], g0[:LANES, span], NN)
+        yield True
+        dk_ref[:, span] = dot(ds[:rows], q0[:LANES, span], NN)
+        yield True
+        o_ref[:, span] = dot(low, stack_rows(v0, v1, head), TN).astype(jnp.bfloat16)
+        yield True
+        part = dot(ds, stack_rows(k0, k1, head), TN) * scale
+        dq_ref[:, span] = part.astype(jnp.bfloat16)
+        yield True
+
+    strips = [("own", head) for head in range(heads)]
+    operands = (q0, k0, v0, g0, None, k1, v1, None)
+    run_strips(strips, rows, operands, lambda kind: bias_ref, outputs)
+
+
+def rest_kernel(
+    heads, rows,
+    s0, s1, own, q1, k1, v1, g1, o_own, dq_own, dk_own, dv_own,
+    o_hbm, dq_hbm, dk_hbm, dv_hbm,
+    bias_ref, o_ref, dq_ref, dk_ref, dv_ref, sem,
+):
+    scale = 1.0 / math.sqrt(HEAD_DIM)
+    q0, k0, v0, g0 = (own.at[at] for at in range(4))
+    own_rest = rows - LANES
+    rest = 2 * own_rest
+
+    for at, (source, target) in enumerate(((o_own, o_hbm), (dq_own, dq_hbm))):
+        pltpu.make_async_copy(source, target.at[:LANES, :], sem.at[at]).start()
+
+    def copy_out(at, head):
+        source, target = (
+            (o_ref, o_hbm.at[LANES:, :]),
+            (dq_ref, dq_hbm.at[LANES:, :]),
+            (dk_ref, dk_hbm),
+            (dv_ref, dv_hbm),
+        )[at]
+        span = cols(head, 2)
+        return pltpu.make_async_copy(source.at[:, span], target.at[:, span], sem.at[at])
+
+    tails = [s0[:, LANES:], s1[:, LANES:]]
+    fill_mask(bias_ref, s0, s1, jnp.concatenate([s1[:, :LANES]] + tails + tails, axis=1))
+
+    def bias_of(kind):
+        return bias_ref[:, :LANES] if kind == "other" else bias_ref[:, LANES:]
+
+    tails_of = {}
+
+    def query_rows(first, second, head):
+        tail = tail_rows(first, second, head)
+        zero = jnp.zeros_like(tail)
+        parts = [second[:LANES, cols(head)]] + ([zero, tail] if head % 2 else [tail, zero])
+        return jnp.concatenate(parts, axis=0)
+
+    def outputs(kind, head, low, ds):
+        if kind == "tail":
+            low_turned, ds_turned = jnp.transpose(low), jnp.transpose(ds)
+            for side in range(2):
+                mine = slice(side * rest, side * rest + own_rest)
+                span = cols(head + side)
+                tails_of[head + side] = (low[:rows], ds[:rows])
+                part = dot(low_turned[mine], stack_rows(v0, v1, head + side), NN)
+                o_ref[:, span] = part.astype(jnp.bfloat16)
+                part = dot(ds_turned[mine], stack_rows(k0, k1, head + side), NN) * scale
+                dq_ref[:, span] = part.astype(jnp.bfloat16)
+                yield True
+            return
+        span = cols(head)
+        low_tail, ds_tail = tails_of.pop(head)
+        part = dot(jnp.concatenate([low, low_tail], axis=1), query_rows(g0, g1, head), NN)
+        dv_ref[:, span] = (part + dv_own[:, span]).astype(jnp.bfloat16)
+        yield True
+        part = dot(jnp.concatenate([ds, ds_tail], axis=1), query_rows(q0, q1, head), NN)
+        dk_ref[:, span] = ((part + dk_own[:, span]) * scale).astype(jnp.bfloat16)
+        if head % 2:
+            for output in range(4):
+                copy_out(output, head - 1).start()
+        yield True
+
+    strips = []
+    for head in range(0, heads, 2):
+        strips += [("tail", head), ("other", head), ("other", head + 1)]
+    run_strips(strips, rows, (q0, k0, v0, g0, q1, k1, v1, g1), bias_of, outputs)
+    for at, target in enumerate((o_hbm, dq_hbm, dk_hbm, dv_hbm)):
+        pltpu.make_async_copy(dk_ref, target, sem.at[at]).wait()
+
+
+def pair_body(queries, key_vectors, values, grad_output, segment_index):
+    rows, width = queries.shape
+    heads = width // HEAD_DIM
+
+    def swap(array):
+        return lax.ppermute(array, "frames", [(0, 1), (1, 0)])
+
+    other_keys, other_values = swap(key_vectors), swap(values)
+    other_segment = swap(segment_index).reshape(1, rows)
+    other_queries, other_grad = swap(queries), swap(grad_output)
+    own, own_segment = load_early(
+        (queries, key_vectors, values, grad_output), segment_index.reshape(1, rows)
+    )
+    on_chip = pl.BlockSpec(memory_space=pltpu.VMEM)
+    f32, bf16 = jnp.float32, jnp.bfloat16
+    limit = 24 * 1024 * 1024
+    partial_results = pl.pallas_call(
+        functools.partial(own_kernel, heads, rows),
+        out_shape=(
+            jax.ShapeDtypeStruct((LANES, width), bf16),
+            jax.ShapeDtypeStruct((LANES, width), bf16),
+            jax.ShapeDtypeStruct((rows, width), f32),
+            jax.ShapeDtypeStruct((rows, width), f32),
+        ),
+        in_specs=[on_chip] * 5,
+        out_specs=(on_chip,) * 4,
+        scratch_shapes=[pltpu.VMEM((2 * rows, LANES), f32)],
+        compiler_params=pltpu.CompilerParams(vmem_limit_bytes=limit),
+        cost_estimate=pl.CostEstimate(
+            flops=12 * LANES * 2 * rows * width,
+            transcendentals=0,
+            bytes_accessed=12 * rows * width * 2,
+        ),
+    )(own_segment, other_segment, own, other_keys, other_values)
+    return pl.pallas_call(
+        functools.partial(rest_kernel, heads, rows),
+        out_shape=(jax.ShapeDtypeStruct((rows, width), bf16),) * 4,
+        in_specs=[on_chip] * 11,
+        out_specs=(pl.BlockSpec(memory_space=pl.ANY),) * 4,
+        scratch_shapes=[pltpu.VMEM((2 * rows, 2 * LANES), f32)]
+        + [pltpu.VMEM((rows - LANES, width), bf16)] * 2
+        + [pltpu.VMEM((rows, width), bf16)] * 2
+        + [pltpu.SemaphoreType.DMA((4,))],
+        compiler_params=pltpu.CompilerParams(vmem_limit_bytes=limit),
+    )(
+        own_segment,
+        other_segment,
+        own,
+        other_queries,
+        other_keys,
+        other_values,
+        other_grad,
+        *partial_results,
+    )
+
+
+def pair_fits(rows, width):
+    return 4 * (rows - LANES) == LANES and width % (2 * HEAD_DIM) == 0
+
+
+def plan_for_shapes(queries, key_vectors, values, grad_output, segment_index):
+    paired = lax.axis_size("frames") == 2 and pair_fits(*queries.shape)
+    body = pair_body if paired else shards
+    return body(queries, key_vectors, values, grad_output, segment_index)
+
+
 def solution(mesh):
     in_specs = (
         P(("dp", "frames"), "heads"),
@@ -221,4 +546,6 @@
         P(("dp", "frames"), "heads"),
         P(("dp", "frames"), "heads"),
     )
-    return jax.shard_map(shards, mesh=mesh, in_specs=in_specs, out_specs=out_specs, check_vma=False)
+    return jax.shard_map(
+        plan_for_shapes, mesh=mesh, in_specs=in_specs, out_specs=out_specs, check_vma=False
+    )

time: 53.2 us -> 9.07 us (0.17)
  blocking collectives: 15.7 us -> 0 us
  matrix products: 14.4 us -> 0 us
  other arithmetic: 9.38 us -> 0 us
  local copies, waits for them, and re-layouts: 8.24 us -> 0 us
  Pallas kernels: 0 us -> 5.93 us
  between operations: 4.77 us -> 0.67 us
  starting transfers between devices: 0 us -> 1.76 us
  waiting for transfers between devices: 0 us -> 0.57 us
    dot_general x7 -> x0, matrix products: 14.4 us -> none  [the longest x3 6.15 us: score_block(): jnp.einsum('qhd,khd->qhk', query_heads, key_heads, preferred_element_type...]
    all_gather x6 -> x0, blocking collectives: 12.9 us -> none  [the longest x1 2.47 us: shards(): lax.all_gather(queries, 'frames', axis=0, tiled=True)]
    unnamed x16 -> x0, local copies, waits for them, and re-layouts: 6.23 us -> none
    pallas_call x0 -> x3, Pallas kernels: none -> 5.93 us  [the longest x1 2.86 us: pair_body(): pl.pallas_call(functools.partial(rest_kernel, heads, rows), out_shape=(ja...]
    convert_element_type x5 -> x0, other arithmetic: 4.21 us -> none  [the longest x1 1.88 us: shards(): (key_acc * scale_factor).reshape(row_count, full_width).astype(jnp.bfloat16)]
    unnamed x1 -> x0, blocking collectives: 2.78 us -> none
    reduce_min x2 -> x0, other arithmetic: 1.9 us -> none  [the longest x1 1.29 us: shards(): own_bottom = jnp.min(own_segment)]
    ppermute x0 -> x5, starting transfers between devices: none -> 1.76 us  [swap(): return lax.ppermute(array, 'frames', [(0, 1), (1, 0)])]
  transfers between devices with their start and end apart: 0 -> 5, of which waited for: 0 -> 1; matrix products, arithmetic and copies ran while one was open for 0% -> 0% of each run, Pallas kernels for 0% -> 34%
where the time goes in v3:
time: 9.07 us; the launch traced here: 8.92 us
  Pallas kernels  5.93 us (65%)
  starting transfers between devices  1.76 us (19%)
  between operations  0.67 us (7%)
  waiting for transfers between devices  0.57 us (6%)
    pallas_call x1, Pallas kernels, pair_body(): pl.pallas_call(functools.partial(rest_kernel, heads, rows), out_shape=(ja...  2.86 us
    pallas_call x1, Pallas kernels, pair_body(): pl.pallas_call(functools.partial(own_kernel, heads, rows), out_shape=(jax...  1.78 us
    ppermute x5, starting transfers between devices, swap(): return lax.ppermute(array, 'frames', [(0, 1), (1, 0)])  1.76 us
    pallas_call x1, Pallas kernels, load_early(): pl.pallas_call(load_kernel, out_shape=(stacked, jax.ShapeDtypeStruct(segm...  1.28 us
    ppermute x5, waiting for transfers between devices, swap(): return lax.ppermute(array, 'frames', [(0, 1), (1, 0)])  0.57 us
  transfers between devices with their start and end apart: 5, of which 1 were waited for; matrix products, arithmetic and copies ran while one was open for 0% of the time, Pallas kernels for 34%

profile of v3, /device:TPU:13, one launch (start us, length us, event | category | flops | bytes accessed | tf_op | source)
XLA Modules:
  0.0 8.9 jit_solution(11235629755138056201)
XLA Ops:
  0.6 0.7 %collective-permute-start.2 = (bf16[160,1024]{1,0:T(8,128)(2,1)}, bf16[160,1024]{1,0:T(8,128)(2,1)S(1)}, u32[]{:S(2)}, u32[]{:S(2)}) collective-permute-start(bf16[160,1024]{1,0:T(8,128)(2,1)} %refs_1_.1), channel_id=1, source_target_pairs={{0,16},{16,0},{1,17},{17,1},{2,18},{18,2},{3,19},{19,3},{4,20},{20... | collective-permute-start | bytes 983048 | tf_op jit(solution)/shard_map/ppermute | solution.py:474
  1.4 0.1 collective-permute-start.3
  1.5 0.4 %collective-permute-start.1 = (bf16[160,1024]{1,0:T(8,128)(2,1)}, bf16[160,1024]{1,0:T(8,128)(2,1)S(1)}, u32[]{:S(2)}, u32[]{:S(2)}) collective-permute-start(bf16[160,1024]{1,0:T(8,128)(2,1)} %refs_0_.1), channel_id=1, source_target_pairs={{0,16},{16,0},{1,17},{17,1},{2,18},{18,2},{3,19},{19,3},{4,20},{20... | collective-permute-start | bytes 983048 | tf_op jit(solution)/shard_map/ppermute | solution.py:474
  1.9 0.1 collective-permute-start.4
  2.0 0.4 %collective-permute-start = (s32[160]{0:T(256)}, s32[160]{0:T(256)S(1)}, u32[]{:S(2)}, u32[]{:S(2)}) collective-permute-start(s32[160]{0:T(256)} %param.9), channel_id=1, source_target_pairs={{0,16},{16,0},{1,17},{17,1},{2,18},{18,2},{3,19},{19,3},{4,20},{20... | collective-permute-start | bytes 1928 | tf_op jit(solution)/shard_map/ppermute | solution.py:474
  2.4 1.3 %shard_map.84 = (bf16[4,160,1024]{2,1,0:T(8,128)(2,1)S(1)}, s32[1,160]{1,0:T(1,128)S(1)}) custom-call(bf16[160,1024]{1,0:T(8,128)(2,1)} %refs_0_.1, bf16[160,1024]{1,0:T(8,128)(2,1)} %refs_1_.1, bf16[160,1024]{1,0:T(8,128)(2,1)} %refs_2_.1, bf16[160,1024]{1,0:T(8,128)(2,1)} %refs_3_.1, s32[1,160]{1,0:T(1,128)} %bitcast.4), custom_call_target="tpu_custom_call" | custom-call | bytes 2621440 | tf_op jit(solution)/shard_map/pallas_call | solution.py:254
  3.7 0.6 %collective-permute-done = s32[160]{0:T(256)S(1)} collective-permute-done((s32[160]{0:T(256)}, s32[160]{0:T(256)S(1)}, u32[]{:S(2)}, u32[]{:S(2)}) %collective-permute-start) | collective-permute-done | bytes 672 | tf_op jit(solution)/shard_map/ppermute | solution.py:474
  4.2 0.0 collective-permute-done.2.k1
  4.2 0.0 collective-permute-done.3.v1
  4.3 1.8 %shard_map.85 = (bf16[128,1024]{1,0:T(8,128)(2,1)S(1)}, bf16[128,1024]{1,0:T(8,128)(2,1)S(1)}, f32[160,1024]{1,0:T(8,128)S(1)}, f32[160,1024]{1,0:T(8,128)S(1)}) custom-call(s32[1,160]{1,0:T(1,128)S(1)} %get-tuple-element.10.s0, s32[1,160]{1,0:T(1,128)S(1)} %bitcast.2, bf16[4,160,1024]{2,1,0:T(8,128)(2,1)S(1)} %get-tuple-element.11.own, ...), custom_call_target="tpu_custom_call" | custom-call | flops 503316480 | bytes 3932160 | tf_op jit(solution)/shard_map/pallas_call | solution.py:485
  6.0 0.0 collective-permute-done.1.q1
  6.0 0.0 collective-permute-done.4.g1
  6.1 2.9 %shard_map.86 = (bf16[160,1024]{1,0:T(8,128)(2,1)}, bf16[160,1024]{1,0:T(8,128)(2,1)}, bf16[160,1024]{1,0:T(8,128)(2,1)}, bf16[160,1024]{1,0:T(8,128)(2,1)}) custom-call(s32[1,160]{1,0:T(1,128)S(1)} %get-tuple-element.10.s0, s32[1,160]{1,0:T(1,128)S(1)} %bitcast.3, bf16[4,160,1024]{2,1,0:T(8,128)(2,1)S(1)} %get-tuple-element.11.own, ...), custom_call_target="tpu_custom_call" | custom-call | tf_op jit(solution)/shard_map/pallas_call | solution.py:503
Async XLA Ops:
  0.6 3.6 %collective-permute-start.2 = (bf16[160,1024]{1,0:T(8,128)(2,1)}, bf16[160,1024]{1,0:T(8,128)(2,1)S(1)}, u32[]{:S(2)}, u32[]{:S(2)}) collective-permute-start(bf16[160,1024]{1,0:T(8,128)(2,1)} %refs_1_.1), channel_id=1, source_target_pairs={{0,16},{16,0},{1,17},{17,1},{2,18},{18,2},{3,19},{19,3},{4,20},{20... | collective-permute-start | bytes 983048 | tf_op jit(solution)/shard_map/ppermute | solution.py:474
  1.4 2.9 %collective-permute-start.3 = (bf16[160,1024]{1,0:T(8,128)(2,1)}, bf16[160,1024]{1,0:T(8,128)(2,1)S(1)}, u32[]{:S(2)}, u32[]{:S(2)}) collective-permute-start(bf16[160,1024]{1,0:T(8,128)(2,1)} %refs_2_.1), channel_id=1, source_target_pairs={{0,16},{16,0},{1,17},{17,1},{2,18},{18,2},{3,19},{19,3},{4,20},{20... | collective-permute-start | bytes 983048 | tf_op jit(solution)/shard_map/ppermute | solution.py:474
  1.5 4.6 %collective-permute-start.1 = (bf16[160,1024]{1,0:T(8,128)(2,1)}, bf16[160,1024]{1,0:T(8,128)(2,1)S(1)}, u32[]{:S(2)}, u32[]{:S(2)}) collective-permute-start(bf16[160,1024]{1,0:T(8,128)(2,1)} %refs_0_.1), channel_id=1, source_target_pairs={{0,16},{16,0},{1,17},{17,1},{2,18},{18,2},{3,19},{19,3},{4,20},{20... | collective-permute-start | bytes 983048 | tf_op jit(solution)/shard_map/ppermute | solution.py:474
  1.9 4.2 %collective-permute-start.4 = (bf16[160,1024]{1,0:T(8,128)(2,1)}, bf16[160,1024]{1,0:T(8,128)(2,1)S(1)}, u32[]{:S(2)}, u32[]{:S(2)}) collective-permute-start(bf16[160,1024]{1,0:T(8,128)(2,1)} %refs_3_.1), channel_id=1, source_target_pairs={{0,16},{16,0},{1,17},{17,1},{2,18},{18,2},{3,19},{19,3},{4,20},{20... | collective-permute-start | bytes 983048 | tf_op jit(solution)/shard_map/ppermute | solution.py:474
  2.0 2.3 %collective-permute-start = (s32[160]{0:T(256)}, s32[160]{0:T(256)S(1)}, u32[]{:S(2)}, u32[]{:S(2)}) collective-permute-start(s32[160]{0:T(256)} %param.9), channel_id=1, source_target_pairs={{0,16},{16,0},{1,17},{17,1},{2,18},{18,2},{3,19},{19,3},{4,20},{20... | collective-permute-start | bytes 1928 | tf_op jit(solution)/shard_map/ppermute | solution.py:474
